TPU v7x, 32 devices: a whole 2x2x4 slice. The times are simulated.
32 devices in a mesh: prow: 8 (over y, x, core), pcol: 4 (over z).
Axes of the slice: x: 2, y: 2, z: 4, core: 2. Of those that a mesh axis runs over, the one named last changes fastest.
Arguments:
- panel: float32 [32768, 512], P('prow', 'pcol'), may hold values from -0.08 to 0.08
- slab: float32 [32768, 2048], P('prow', 'pcol'), may hold values from -6 to 6
- pivots: int32 [512], replicated, may hold values from 512 to 32767, as said below
- diag_inverse: float32 [512, 512], replicated, as said below
Outputs:
- updated: float32 [32768, 2048], P('prow', 'pcol')
Inputs may be any that keep to these rules, and one draw needn't show every extreme that they name: `pivots`: 512 distinct row indices, each below the diagonal block; their owners along prow are uneven. `diag_inverse`: unit lower triangular.
All inputs are finite; a program needn't handle non-finite values.
Results may differ from a plain program's by a relative error of at most 0.000053.
Values sent between devices are 32-bit elements; how exact they have to be, the bound alone decides.
No kernel may reach another device: no remote copies, remote signals or barrier semaphores. Data moves between devices by JAX's collectives and lax.ppermute only.
A program may use at most 128 MiB of HBM per device.

v0:
```python
import jax
import jax.numpy as jnp
from jax import lax
from jax.sharding import PartitionSpec as P


def from_root(value, axis, source):
    kept = jnp.where(lax.axis_index(axis) == source, value, 0).astype(value.dtype)
    return lax.psum(kept, axis)


def shards(panel, slab, pivots, diag_inverse):
    rows_here = slab.shape[0]
    width_here = slab.shape[1]
    block_size = diag_inverse.shape[0]
    first_row = lax.axis_index("prow") * rows_here
    local_row = pivots - first_row
    owned = (local_row >= 0) & (local_row < rows_here)
    safe_row = jnp.clip(local_row, 0, rows_here - 1)
    picked = jnp.where(owned[:, None], slab[safe_row], 0.0)
    top_block = lax.psum(picked, "prow")
    upper = jnp.dot(
        diag_inverse, top_block, precision=lax.Precision.HIGHEST, preferred_element_type=jnp.float32
    )
    old_top = from_root(slab[:block_size], "prow", 0)
    target_row = jnp.where(owned, local_row, rows_here)
    swapped = slab.at[target_row].set(old_top, mode="drop")
    product = jnp.dot(
        lax.all_gather(panel, "pcol", axis=1, tiled=True),
        upper,
        precision=lax.Precision.HIGHEST,
        preferred_element_type=jnp.float32,
    )
    updated = swapped - product
    global_row = first_row + jnp.arange(rows_here, dtype=jnp.int32)
    upper_padded = jnp.concatenate(
        [upper, jnp.zeros((rows_here - block_size, width_here), jnp.float32)], axis=0
    )
    return jnp.where((global_row < block_size)[:, None], upper_padded, updated)


def solution(mesh):
    in_specs = (P("prow", "pcol"), P("prow", "pcol"), P(), P())
    out_specs = P("prow", "pcol")
    return jax.shard_map(shards, mesh=mesh, in_specs=in_specs, out_specs=out_specs, check_vma=False)
```

profile of v0, /device:TPU:0, one launch (start us, length us, event | category | flops | bytes accessed | tf_op | source)
XLA Modules:
  0.0 213.0 jit_solution(16660323267572027275)
XLA Ops:
  7.4 0.0 copy-start
  7.4 0.0 copy-start.2
  7.4 0.0 all-reduce.4.cloned.1.call-start
  7.4 7.9 %copy.11 = f32[4096,512]{1,0:T(8,128)} copy(f32[4096,512]{1,0:T(8,128)} %param.5) | data formatting | bytes 16777216
  15.2 0.0 copy-done.2
  15.3 5.4 %gather_fusion = f32[512,512]{1,0:T(8,128)S(1)} fusion(f32[4096,512]{1,0:T(8,128)} %copy.11, s32[1024]{0:T(1024)S(1)} %pad_clamp_fusion), kind=kCustom, calls=%fused_computation | custom fusion | bytes 2099200 | tf_op jit(solution)/shard_map/gather | solution.py:20
  20.7 2.8 %slice_select_fusion = (f32[512,512]{1,0:T(8,128)}, f32[512,512]{1,0:T(8,128)}) fusion(f32[4096,512]{1,0:T(8,128)} %copy.11, pred[]{:T(512)S(6)} %eq.3, f32[512,512]{1,0:T(8,128)S(1)} %gather_fusion, pred[512]{0:T(512)(128)(4,1)S(1)} %compare_and_fusion), kind=kLoop, calls=%fused_computation.4 | loop fusion | flops 524288 | bytes 4194817 | tf_op jit(solution)/shard_map/jit(_where)/select_n | solution.py:8
  23.5 0.0 all-reduce.4.cloned.1.call-update
  23.5 0.0 all-gather.2.cloned.1.call-start
  23.5 0.5 all-gather.2.cloned.1.call-update
  24.1 63.8 %all-reduce.4.cloned.1.call-done = (f32[512,512]{1,0:T(8,128)}, f32[512,512]{1,0:T(8,128)}) async-done(((f32[512,512]{1,0:T(8,128)}, f32[512,512]{1,0:T(8,128)}), (f32[512,512]{1,0:T(8,128)}, f32[512,512]{1,0:T(8,128)})) %all-reduce.4.cloned.1.call-update) | async-done | bytes 2097168 | tf_op jit(solution)/shard_map/psum | solution.py:9
  87.9 9.7 %scatter_fusion = f32[4096,512]{1,0:T(8,128)} fusion(f32[4096,512]{1,0:T(8,128)} %copy.11, s32[512]{0:T(512)S(1)} %get-tuple-element.8, f32[512,512]{1,0:T(8,128)} %get-tuple-element.5), kind=kCustom, calls=%fused_computation.1 | custom fusion | bytes 3147776 | tf_op jit(solution)/shard_map/scatter | solution.py:27
  97.6 0.0 copy-start.1
  97.6 9.0 %copy.5 = f32[4096,512]{0,1:T(8,128)} copy(f32[4096,512]{1,0:T(8,128)} %scatter_fusion) | data formatting | bytes 16777216 | tf_op jit(solution)/shard_map/scatter | solution.py:27
  106.7 0.0 copy-done
  106.7 0.0 copy-done.1
  106.7 3.5 %fusion.1 = f32[512,512]{1,0:T(8,128)S(1)} fusion(f32[512,512]{1,0:T(8,128)S(1)} %copy-done.1, f32[512,512]{1,0:T(8,128)S(1)} %copy-done), kind=kOutput, calls=%fused_computation.11 | convolution fusion | flops 1610612736 | bytes 3145728 | tf_op jit(solution)/shard_map/dot_general | solution.py:22
  110.1 67.1 %all-gather.2.cloned.1.call-done = f32[4096,512]{1,0:T(8,128)} async-done(((f32[4096,128]{1,0:T(8,128)}), f32[4096,512]{1,0:T(8,128)}) %all-gather.2.cloned.1.call-update) | async-done | bytes 8388624 | tf_op jit(solution)/shard_map/all_gather | solution.py:29
  177.2 19.4 %fusion = f32[4096,512]{0,1:T(8,128)} fusion(f32[4096,512]{0,1:T(8,128)} %copy.5, f32[512,512]{0,1:T(8,128)S(1)} %bitcast.9, f32[512,512]{1,0:T(8,128)S(1)} %fusion.1, f32[4096,512]{1,0:T(8,128)} %all-gather.2.cloned.1.call-done, pred[4096]{0:T(1024)(128)(4,1)S(1)} %add_compare_fusion), kind=kOutput, calls=%fused_computation.3 | convolution fusion | flops 12889096192 | bytes 27267072 | tf_op jit(solution)/shard_map/dot_general | solution.py:28
  196.6 8.9 %copy.6 = f32[4096,512]{1,0:T(8,128)} copy(f32[4096,512]{0,1:T(8,128)} %fusion) | data formatting | bytes 16777216 | tf_op jit(solution)/shard_map/jit(_where)/select_n | solution.py:39
  (4 shorter events, 0.0 us)
Async XLA Ops:
  7.4 99.3 %copy-start = (f32[512,512]{1,0:T(8,128)S(1)}, f32[512,512]{1,0:T(8,128)}, u32[]{:S(2)}) copy-start(f32[512,512]{1,0:T(8,128)} %param.7) | copy-start | bytes 3145732
  7.4 7.9 %copy-start.2 = (s32[512]{0:T(512)S(1)}, s32[512]{0:T(512)}, u32[]{:S(2)}) copy-start(s32[512]{0:T(512)} %param.6) | copy-start | bytes 6148
  7.4 80.5 %all-reduce.4.cloned.1.call-start = ((), (), s32[]{:S(2)}) async-start(), calls=%async_computation.1 | async-start | bytes 4194304 | tf_op jit(solution)/shard_map/psum | solution.py:9
  23.5 153.7 %all-gather.2.cloned.1.call-start = ((), (), s32[]{:S(2)}) async-start(), calls=%async_computation | async-start | bytes 10485760 | tf_op jit(solution)/shard_map/all_gather | solution.py:29
  97.6 9.1 %copy-start.1 = (f32[512,512]{1,0:T(8,128)S(1)}, f32[512,512]{1,0:T(8,128)}, u32[]{:S(2)}) copy-start(f32[512,512]{1,0:T(8,128)} %get-tuple-element.6) | copy-start | bytes 3145732
Sparse Core Ops, SparseCore 0:
  23.6 64.2 all-reduce.3
Sparse Core Ops, SparseCore 1:
  25.5 151.6 all-gather.1
where the time goes:
time: 214 us; the launch traced here: 213 us
  waiting for transfers between devices  131 us (61%)
  local copies, waits for them, and re-layouts  41 us (19%)
  matrix products  22.8 us (11%)
  between operations  14.9 us (7%)
  other arithmetic  2.79 us (1%)
    all_gather x1, waiting for transfers between devices, shards(): lax.all_gather(panel, 'pcol', axis=1, tiled=True)  67.1 us
    psum x1, waiting for transfers between devices, from_root(): return lax.psum(kept, axis)  63.8 us
    dot_general x1, matrix products, shards(): jnp.dot(lax.all_gather(panel, 'pcol', axis=1, tiled=True), upper, precisi...  19.4 us
    scatter x2, local copies, waits for them, and re-layouts, shards(): swapped = slab.at[target_row].set(old_top, mode='drop')  18.8 us
    select_n x1, local copies, waits for them, and re-layouts, shards(): return jnp.where((global_row < block_size)[:, None], upper_padded, updated)  8.94 us
    unnamed x7, local copies, waits for them, and re-layouts  7.87 us
    gather x1, local copies, waits for them, and re-layouts, shards(): picked = jnp.where(owned[:, None], slab[safe_row], 0.0)  5.41 us
  transfers between devices with their start and end apart: 2, of which 2 were waited for; matrix products, arithmetic and copies ran while one was open for 10% of the time, Pallas kernels for 0%

commit v1 on v0

--- a/solution.py
+++ b/solution.py
@@ -6,7 +6,7 @@
 
 def from_root(value, axis, source):
     kept = jnp.where(lax.axis_index(axis) == source, value, 0).astype(value.dtype)
-    return lax.psum(kept, axis)
+    return jnp.sum(lax.all_gather(kept, axis), 0)
 
 
 def shards(panel, slab, pivots, diag_inverse):

time: 214 us -> 322 us (1.50)
  waiting for transfers between devices: 131 us -> 236 us
  other arithmetic: 2.79 us -> 7.99 us
    all_gather x1, waiting for transfers between devices: 67.1 us -> 128 us  [shards(): lax.all_gather(panel, 'pcol', axis=1, tiled=True)]
    all_gather x0 -> x1, waiting for transfers between devices: none -> 50.7 us  [from_root(): return jnp.sum(lax.all_gather(kept, axis), 0)]
    psum x1, waiting for transfers between devices: 63.8 us -> 56.3 us  [shards(): top_block = lax.psum(picked, 'prow')]
    reduce_sum x0 -> x1, other arithmetic: none -> 4.49 us  [from_root(): return jnp.sum(lax.all_gather(kept, axis), 0)]
  transfers between devices with their start and end apart: 2 -> 3, of which waited for: 2 -> 3; matrix products, arithmetic and copies ran while one was open for 10% -> 9% of each run, Pallas kernels for 0% -> 0%
where the time goes in v1:
time: 322 us; the launch traced here: 321 us
  waiting for transfers between devices  236 us (73%)
  local copies, waits for them, and re-layouts  40.2 us (12%)
  matrix products  24 us (7%)
  between operations  13.2 us (4%)
  other arithmetic  7.99 us (2%)
    all_gather x1, waiting for transfers between devices, shards(): lax.all_gather(panel, 'pcol', axis=1, tiled=True)  128 us
    psum x1, waiting for transfers between devices, shards(): top_block = lax.psum(picked, 'prow')  56.3 us
    all_gather x1, waiting for transfers between devices, from_root(): return jnp.sum(lax.all_gather(kept, axis), 0)  50.7 us
    dot_general x1, matrix products, shards(): jnp.dot(lax.all_gather(panel, 'pcol', axis=1, tiled=True), upper, precisi...  19.3 us
    scatter x2, local copies, waits for them, and re-layouts, shards(): swapped = slab.at[target_row].set(old_top, mode='drop')  18 us
    select_n x1, local copies, waits for them, and re-layouts, shards(): return jnp.where((global_row < block_size)[:, None], upper_padded, updated)  8.94 us
    unnamed x7, local copies, waits for them, and re-layouts  7.87 us
  transfers between devices with their start and end apart: 3, of which 3 were waited for; matrix products, arithmetic and copies ran while one was open for 9% of the time, Pallas kernels for 0%

profile of v1, /device:TPU:0, one launch (start us, length us, event | category | flops | bytes accessed | tf_op | source)
XLA Modules:
  0.0 321.4 jit_solution(14522470752486539905)
XLA Ops:
  6.5 0.0 copy-start
  6.5 0.0 copy-start.2
  6.5 0.0 all-reduce.3.cloned.1.call-start
  6.5 7.9 %copy.10 = f32[4096,512]{1,0:T(8,128)} copy(f32[4096,512]{1,0:T(8,128)} %param.5) | data formatting | bytes 16777216
  14.4 0.0 copy-done.2
  14.4 5.4 %gather_fusion = f32[512,512]{1,0:T(8,128)S(1)} fusion(f32[4096,512]{1,0:T(8,128)} %copy.10, s32[1024]{0:T(1024)S(1)} %pad_clamp_fusion), kind=kCustom, calls=%fused_computation | custom fusion | bytes 2099200 | tf_op jit(solution)/shard_map/gather | solution.py:20
  19.9 1.1 broadcast_select_fusion
  21.0 0.0 all-reduce.3.cloned.1.call-update
  21.0 0.0 all-gather.6.cloned.1.call-start
  21.1 2.3 slice_select_fusion
  23.4 0.0 all-gather.6.cloned.1.call-update
  23.4 0.0 all-gather.4.cloned.1.call-start
  23.5 0.7 all-gather.4.cloned.1.call-update
  24.2 56.3 %all-reduce.3.cloned.1.call-done = f32[512,512]{1,0:T(8,128)} async-done(((f32[512,512]{1,0:T(8,128)}), f32[512,512]{1,0:T(8,128)}) %all-reduce.3.cloned.1.call-update) | async-done | bytes 1048592 | tf_op jit(solution)/shard_map/psum | solution.py:21
  80.5 0.0 copy-done
  80.5 4.7 %fusion.1 = f32[512,512]{1,0:T(8,128)S(1)} fusion(f32[512,512]{1,0:T(8,128)} %all-reduce.3.cloned.1.call-done, f32[512,512]{1,0:T(8,128)S(1)} %copy-done), kind=kOutput, calls=%fused_computation.11 | convolution fusion | flops 1610612736 | bytes 3145728 | tf_op jit(solution)/shard_map/dot_general | solution.py:22
  85.2 50.7 %all-gather.6.cloned.1.call-done = f32[4096,512]{1,0:T(8,128)} async-done(((f32[512,512]{1,0:T(8,128)}), f32[4096,512]{1,0:T(8,128)}) %all-gather.6.cloned.1.call-update) | async-done | bytes 8388624 | tf_op jit(solution)/shard_map/all_gather | solution.py:9
  135.8 4.5 %reduce_sum.9 = f32[512,512]{1,0:T(8,128)S(1)} reduce(f32[8,512,512]{2,1,0:T(8,128)} %bitcast.11, f32[]{:T(128)} %constant.6.clone.1), dimensions={0}, to_apply=%region_1.2 | reduce | flops 1835008 | bytes 9437188 | tf_op jit(solution)/shard_map/reduce_sum | solution.py:9
  140.3 9.0 %scatter_fusion = f32[4096,512]{1,0:T(8,128)} fusion(f32[4096,512]{1,0:T(8,128)} %copy.10, s32[512]{0:T(512)S(1)} %get-tuple-element.6, f32[512,512]{1,0:T(8,128)S(1)} %reduce_sum.9), kind=kCustom, calls=%fused_computation.1 | custom fusion | bytes 3147776 | tf_op jit(solution)/shard_map/scatter | solution.py:27
  149.3 9.0 %copy.5 = f32[4096,512]{0,1:T(8,128)} copy(f32[4096,512]{1,0:T(8,128)} %scatter_fusion) | data formatting | bytes 16777216 | tf_op jit(solution)/shard_map/scatter | solution.py:27
  158.3 128.3 %all-gather.4.cloned.1.call-done = f32[4096,512]{1,0:T(8,128)} async-done(((f32[4096,128]{1,0:T(8,128)}), f32[4096,512]{1,0:T(8,128)}) %all-gather.4.cloned.1.call-update) | async-done | bytes 8388624 | tf_op jit(solution)/shard_map/all_gather | solution.py:29
  286.6 0.0 copy-start.1
  286.6 19.3 %fusion = f32[4096,512]{0,1:T(8,128)} fusion(f32[4096,512]{0,1:T(8,128)} %copy.5, f32[512,512]{0,1:T(8,128)S(1)} %bitcast.10, f32[512,512]{1,0:T(8,128)S(1)} %fusion.1, f32[4096,512]{1,0:T(8,128)} %all-gather.4.cloned.1.call-done, pred[4096]{0:T(1024)(128)(4,1)S(1)} %add_compare_fusion), kind=kOutput, calls=%fused_computation.3 | convolution fusion | flops 12889096192 | bytes 27267072 | tf_op jit(solution)/shard_map/dot_general | solution.py:28
  305.9 8.9 %copy.6 = f32[4096,512]{1,0:T(8,128)} copy(f32[4096,512]{0,1:T(8,128)} %fusion) | data formatting | bytes 16777216 | tf_op jit(solution)/shard_map/jit(_where)/select_n | solution.py:39
  314.8 0.0 copy-done.1
  (4 shorter events, 0.0 us)
Async XLA Ops:
  6.5 73.9 %copy-start = (f32[512,512]{1,0:T(8,128)S(1)}, f32[512,512]{1,0:T(8,128)}, u32[]{:S(2)}) copy-start(f32[512,512]{1,0:T(8,128)} %param.7) | copy-start | bytes 3145732
  6.5 7.9 %copy-start.2 = (s32[512]{0:T(512)S(1)}, s32[512]{0:T(512)}, u32[]{:S(2)}) copy-start(s32[512]{0:T(512)} %param.6) | copy-start | bytes 6148
  6.5 73.9 %all-reduce.3.cloned.1.call-start = ((), (), s32[]{:S(2)}) async-start(), calls=%async_computation | async-start | bytes 2097152 | tf_op jit(solution)/shard_map/psum | solution.py:21
  21.0 114.8 %all-gather.6.cloned.1.call-start = ((), (), s32[]{:S(2)}) async-start(), calls=%async_computation.2 | async-start | bytes 9437184 | tf_op jit(solution)/shard_map/all_gather | solution.py:9
  23.4 263.1 %all-gather.4.cloned.1.call-start = ((), (), s32[]{:S(2)}) async-start(), calls=%async_computation.1 | async-start | bytes 10485760 | tf_op jit(solution)/shard_map/all_gather | solution.py:29
  286.6 28.3 %copy-start.1 = (f32[512,512]{1,0:T(8,128)S(1)}, f32[512,512]{1,0:T(8,128)}, u32[]{:S(2)}) copy-start(f32[512,512]{1,0:T(8,128)} %param.7) | copy-start | bytes 3145732
Sparse Core Ops, SparseCore 0:
  21.1 59.2 all-reduce.2
  82.4 53.4 all-gather.5
  137.4 149.1 all-gather.3
